TPU v7x, 128 devices: a whole 4x4x4 slice. The times are simulated.
128 devices in a mesh: gx: 64 (over y, x, z_hi, core), gy: 2 (over z_lo).
Axes of the slice: x: 4, y: 4, z: 4 (z_hi: 2, z_lo: 2; z = z_hi * 2 + z_lo), core: 2. Of those that a mesh axis runs over, the one named last changes fastest.
Arguments:
- adjoint_in: float32 [3, 1024, 128, 256], P(None, 'gx', 'gy'), may hold values from -6 to 6
- checkpoints: bfloat16 [2, 16384, 3, 2048], P(None, ('gx', 'gy')), may hold values from -4 to 4
- send_owner: int32 [16384], P(('gx', 'gy')), may hold values from 0 to 127, as said below
- receive_rows: int32 [16384], P(('gx', 'gy')), may hold values from 0 to 255, as said below
- block_columns: int32 [4096, 8], P(('gx', 'gy')), may hold values from 0 to 35
- eddy_blocks: bfloat16 [8, 128, 128], replicated, may hold values from -0.1875 to 0.1875
- thrust: float32 [80], replicated, may hold values from 0.4 to 1
- yaw_angle: float32 [80], replicated, may hold values from -0.5 to 0.5
- turbine_place: float32 [3, 80], replicated, may hold values from 0 to 1
- turbine_tile: int32 [80], replicated, may hold values from 0 to 127
- fringe_rows: int32 [128], replicated, may hold values from 0 to 1023, as said below
Outputs:
- adjoint_out: float32 [3, 1024, 128, 256], P(None, 'gx', 'gy')
- control_gradient: float32 [2, 80], replicated
Inputs may be any that keep to these rules, and one draw needn't show every extreme that they name: `send_owner`: each storage tile holds 128 slots; at most 2 of its slots name one owner, exactly 2 for some owners; every owner is named by 128 slots in all. `receive_rows`: for each owner the 128 entries name each row storage*2+rank of a slot sent to it exactly once. `fringe_rows`: distinct rows.
All inputs are finite; a program needn't handle non-finite values.
Results may differ from a plain program's by a relative error of at most 0.00086.
Values may be sent and summed in bfloat16 or wider, within the bound.
A program may use at most 128 MiB of HBM per device.

v0:
```python
import jax
import jax.numpy as jnp
from jax import lax
from jax.sharding import PartitionSpec as P

PB = 128
KB = 8
CAP = 2
NZB = 2
TIME_STEP = 0.25
BASE_VISC = 0.1
EDDY_COEF = 0.5
KERNEL_WIDTH = 1.5
FRINGE_KEEP = 0.5


def padded(block, sides, width):
    for axis, dim in sides:
        count = lax.axis_size(axis)
        forward = [(i, i + 1) for i in range(count - 1)]
        forward.append((count - 1, 0))
        backward = [(target, source) for source, target in forward]
        low = lax.ppermute(
            lax.slice_in_dim(block, block.shape[dim] - width, None, axis=dim), axis, forward
        )
        high = lax.ppermute(lax.slice_in_dim(block, 0, width, axis=dim), axis, backward)
        block = jnp.concatenate([low, block, high], axis=dim)
    return block


def turbine_terms(
    tile_index, thrust, yaw_angle, turbine_place, turbine_tile, width_x, width_y, height
):
    owned_mask = (turbine_tile == tile_index).astype(jnp.float32)
    spread = 2.0 * KERNEL_WIDTH * KERNEL_WIDTH
    along_x = jnp.exp(
        -(
            (jnp.arange(width_x, dtype=jnp.float32)[None, :] - turbine_place[0][:, None] * width_x)
            ** 2
        )
        / spread
    )
    along_y = jnp.exp(
        -(
            (jnp.arange(width_y, dtype=jnp.float32)[None, :] - turbine_place[1][:, None] * width_y)
            ** 2
        )
        / spread
    )
    along_z = jnp.exp(
        -(
            (
                jnp.arange(height, dtype=jnp.float32)[None, :]
                - turbine_place[2][:, None] * (0.5 * height)
            )
            ** 2
        )
        / spread
    )
    plan_kernel = (along_x[:, :, None] * along_y[:, None, :]).reshape(
        along_x.shape[0], width_x * width_y
    )
    cosine = jnp.cos(yaw_angle)
    loading = owned_mask * thrust * cosine * cosine
    drag_field = jnp.dot(
        (plan_kernel * loading[:, None]).T, along_z, precision=lax.Precision.HIGHEST
    )
    return (owned_mask, plan_kernel, along_z, drag_field.reshape(width_x, width_y, height))


def block_selector(columns, width_x):
    count_in = (width_x + 2) * NZB
    picks = (columns[:, :, None] == jnp.arange(count_in, dtype=jnp.int32)[None, None, :]).astype(
        jnp.bfloat16
    )
    return picks.reshape(width_x, NZB, KB, width_x + 2, NZB)


def advance(
    extended,
    forward,
    selector,
    eddy_blocks,
    owned_mask,
    plan_kernel,
    along_z,
    drag_field,
    fringe_scale,
):
    center = extended[:, 1:-1, 1:-1, :]
    east_cells = extended[:, 2:, 1:-1, :]
    west_cells = extended[:, :-2, 1:-1, :]
    north_cells = extended[:, 1:-1, 2:, :]
    south_cells = extended[:, 1:-1, :-2, :]
    zero_plane = jnp.zeros_like(center[..., :1])
    upper_cells = jnp.concatenate([center[..., 1:], zero_plane], axis=3)
    lower_cells = jnp.concatenate([zero_plane, center[..., :-1]], axis=3)
    velocity = forward.astype(jnp.float32)
    laplace = (
        east_cells
        + west_cells
        + north_cells
        + south_cells
        + upper_cells
        + lower_cells
        - 6.0 * center
    )
    advect = 0.5 * (
        velocity[0] * (east_cells - west_cells)
        + velocity[1] * (north_cells - south_cells)
        + velocity[2] * (upper_cells - lower_cells)
    )
    viscous = EDDY_COEF * jnp.sqrt(1.0 + jnp.sum(velocity * velocity, axis=0))
    components, width_x, width_y, height = center.shape
    planes = extended[:, :, 1:-1, :].astype(jnp.bfloat16)
    planes = planes.reshape(components, width_x + 2, width_y, NZB, PB)
    picked = jnp.einsum(
        "xbkqc,aqycz->xbkayz", selector, planes, preferred_element_type=jnp.float32
    ).astype(jnp.bfloat16)
    product = jnp.einsum(
        "xbkayz,kzw->axybw", picked, eddy_blocks, preferred_element_type=jnp.float32
    )
    product = product.reshape(components, width_x, width_y, height)
    update = center + TIME_STEP * (advect + BASE_VISC * laplace + viscous * product)
    drag_term = TIME_STEP * drag_field * velocity[0] * center[0]
    first_only = (jnp.arange(components, dtype=jnp.int32) == 0).astype(jnp.float32)
    update = update - first_only[:, None, None, None] * drag_term[None]
    update = update * fringe_scale[None, :, None, None]
    density = (velocity[0] * velocity[0] * center[0]).reshape(width_x * width_y, height)
    projected = jnp.dot(density, along_z.T, precision=lax.Precision.HIGHEST)
    gradient_part = owned_mask * jnp.sum(plan_kernel.T * projected, axis=0)
    return (update, gradient_part)


def shards(
    adjoint_in,
    checkpoints,
    send_owner,
    receive_rows,
    block_columns,
    eddy_blocks,
    thrust,
    yaw_angle,
    turbine_place,
    turbine_tile,
    fringe_rows,
):
    count_x = lax.axis_size("gx")
    count_y = lax.axis_size("gy")
    tile_count = count_x * count_y
    tile_index = lax.axis_index("gx") * count_y + lax.axis_index("gy")
    components, width_x, width_y, height = adjoint_in.shape
    steps_total = checkpoints.shape[0]
    block_shape = checkpoints.shape[2:]
    owner_ids = jnp.arange(tile_count, dtype=jnp.int32)
    onehot = (send_owner[:, None] == owner_ids[None, :]).astype(jnp.int32)
    slot_rank = jnp.sum(jnp.cumsum(onehot, axis=0) * onehot, axis=1) - 1
    position = send_owner * CAP + slot_rank
    row_ids = jnp.arange(tile_count * CAP, dtype=jnp.int32)
    pack_table = (row_ids[:, None] == position[None, :]).astype(jnp.bfloat16)
    pick_table = (receive_rows[:, None] == row_ids[None, :]).astype(jnp.bfloat16)
    selector = block_selector(block_columns, width_x)
    rows_x = lax.axis_index("gx") * width_x + jnp.arange(width_x, dtype=jnp.int32)
    fringe_hit = jnp.any(rows_x[:, None] == fringe_rows[None, :], axis=1)
    fringe_scale = jnp.where(fringe_hit, FRINGE_KEEP, 1.0).astype(jnp.float32)
    owned_mask, plan_kernel, along_z, drag_field = turbine_terms(
        tile_index, thrust, yaw_angle, turbine_place, turbine_tile, width_x, width_y, height
    )
    adjoint = adjoint_in
    gradient_sum = jnp.zeros((thrust.shape[0],), jnp.float32)
    for step_index in range(steps_total):
        stored = checkpoints[steps_total - 1 - step_index]
        packed = jnp.einsum(
            "rs,scb->rcb", pack_table, stored, preferred_element_type=jnp.float32
        ).astype(jnp.bfloat16)
        arrived = lax.all_to_all(
            packed.reshape((tile_count, CAP) + block_shape),
            ("gx", "gy"),
            split_axis=0,
            concat_axis=0,
            tiled=True,
        )
        arrived = arrived.reshape((tile_count * CAP,) + block_shape)
        forward = jnp.einsum(
            "jr,rcb->cjb", pick_table, arrived, preferred_element_type=jnp.float32
        ).astype(jnp.bfloat16)
        forward = forward.reshape(components, width_x, width_y, height)
        extended = padded(adjoint, (("gx", 1), ("gy", 2)), 1)
        adjoint, gradient_part = advance(
            extended,
            forward,
            selector,
            eddy_blocks,
            owned_mask,
            plan_kernel,
            along_z,
            drag_field,
            fringe_scale,
        )
        gradient_sum = gradient_sum + lax.psum(gradient_part, ("gx", "gy"))
    cosine = jnp.cos(yaw_angle)
    sine = jnp.sin(yaw_angle)
    control_gradient = jnp.stack(
        [
            -0.5 * TIME_STEP * cosine * cosine * gradient_sum,
            TIME_STEP * thrust * sine * cosine * gradient_sum,
        ]
    )
    return (adjoint, control_gradient)


def solution(mesh):
    return jax.shard_map(
        shards,
        mesh=mesh,
        in_specs=(
            P(None, "gx", "gy", None),
            P(None, ("gx", "gy"), None, None),
            P(("gx", "gy")),
            P(("gx", "gy")),
            P(("gx", "gy"), None),
            P(),
            P(),
            P(),
            P(),
            P(),
            P(),
        ),
        out_specs=(P(None, "gx", "gy", None), P()),
        check_vma=False,
    )
```

profile of v0, /device:TPU:1, one launch (start us, length us, event | category | flops | bytes accessed | tf_op | source)
XLA Modules:
  0.0 342.7 jit_solution(4182224922127656898)
XLA Ops:
  3.1 4.0 %convolution_convert_fusion.1 = bf16[256,3,2048]{2,0,1:T(8,128)(2,1)} fusion(bf16[2,128,3,2048]{3,1,2,0:T(8,128)(2,1)} %param.12, s32[128]{0:T(128)S(1)} %add_add_fusion), kind=kOutput, calls=%fused_computation.11 | convolution fusion | flops 404258816 | bytes 4719104 | tf_op jit(solution)/shard_map/rs,scb->rcb/dot_general | solution.py:173
  7.1 4.6 %reshape.194 = bf16[128,2,3,2048]{3,1,0,2:T(2,128)(2,1)S(1)} reshape(bf16[256,3,2048]{2,0,1:T(8,128)(2,1)} %convolution_convert_fusion.1) | data formatting | bytes 6291456 | tf_op jit(solution)/shard_map/reshape | solution.py:177
  11.7 3.8 %copy.121 = bf16[128,2,3,2048]{3,1,2,0:T(2,128)(2,1)} copy(bf16[128,2,3,2048]{3,1,0,2:T(2,128)(2,1)S(1)} %reshape.194) | data formatting | bytes 6291456 | tf_op jit(solution)/shard_map/reshape | solution.py:177
  15.6 11.9 %all-to-all-start = ((bf16[128,2,3,2048]{3,1,2,0:T(2,128)(2,1)}), bf16[128,2,3,2048]{3,1,2,0:T(2,128)(2,1)}, u32[]{:S(2)}, u32[]{:S(2)}) async-start(bf16[128,2,3,2048]{3,1,2,0:T(2,128)(2,1)} %copy.121), calls=%async_computation | async-start | bytes 6291456 | tf_op jit(solution)/shard_map/all_to_all | solution.py:176
  28.3 3.5 %collective-permute-start.1 = (f32[3,1,64,256]{3,2,1,0:T(8,128)}, f32[3,1,64,256]{3,2,1,0:T(8,128)}, u32[]{:S(2)}, u32[]{:S(2)}) collective-permute-start(f32[3,1,64,256]{3,2,1,0:T(8,128)} %get-tuple-element.24), channel_id=1, source_target_pairs={{0,2},{2,4},{4,6},{6,8},{8,10},{10,12},{12,14},{14,16},{16,18},{18... | collective-permute-start | bytes 589832 | tf_op jit(solution)/shard_map/ppermute | solution.py:23
  32.0 3.8 %fusion.65 = (f32[3,16,64,255]{3,2,1,0:T(8,128)}, f32[3,16,64,255]{3,2,1,0:T(8,128)}) fusion(f32[3,16,64,256]{3,2,1,0:T(8,128)S(1)} %copy-done.1), kind=kLoop, calls=%fused_computation.124 | loop fusion | bytes 12533760 | tf_op jit(solution)/shard_map/slice | solution.py:96
  45.7 6.0 %reshape.197 = bf16[128,2,3,2048]{3,1,0,2:T(2,128)(2,1)} reshape(bf16[256,3,2048]{2,0,1:T(8,128)(2,1)} %convolution_convert_fusion) | data formatting | bytes 6291456 | tf_op jit(solution)/shard_map/reshape | solution.py:177
  51.7 5.7 %copy.136 = bf16[128,2,3,2048]{3,1,2,0:T(2,128)(2,1)} copy(bf16[128,2,3,2048]{3,1,0,2:T(2,128)(2,1)} %reshape.197) | data formatting | bytes 6291456 | tf_op jit(solution)/shard_map/reshape | solution.py:177
  57.6 8.9 %collective-permute-done.1 = f32[3,1,64,256]{3,2,1,0:T(8,128)} collective-permute-done((f32[3,1,64,256]{3,2,1,0:T(8,128)}, f32[3,1,64,256]{3,2,1,0:T(8,128)}, u32[]{:S(2)}, u32[]{:S(2)}) %collective-permute-start.1) | collective-permute-done | bytes 196640 | tf_op jit(solution)/shard_map/ppermute | solution.py:23
  74.2 3.5 %concatenate.72 = bf16[3,16,64,2,128]{4,3,2,1,0:T(2,128)(2,1)} reshape(bf16[3,16,64,256]{3,2,1,0:T(8,128)(2,1)} %get-tuple-element.21) | data formatting | bytes 3145728 | tf_op jit(solution)/shard_map/concatenate | solution.py:27
  77.7 4.4 %copy.130 = bf16[3,16,64,2,128]{4,1,3,2,0:T(8,128)(2,1)} copy(bf16[3,16,64,2,128]{4,3,2,1,0:T(2,128)(2,1)} %concatenate.72) | data formatting | bytes 3145728 | tf_op jit(solution)/shard_map/concatenate | solution.py:27
  82.8 5.6 %bitcast_convert_fusion.1 = bf16[16,2,8,3,64,128]{5,2,4,3,1,0:T(8,128)(2,1)S(1)} fusion(bf16[3,1,64,2,128]{4,1,3,2,0:T(2,128)(2,1)} %concatenate.87, bf16[3,16,64,2,128]{4,1,3,2,0:T(8,128)(2,1)} %copy.130, bf16[3,1,64,2,128]{4,1,3,2,0:T(2,128)(2,1)} %concatenate.86, s32[18,2]{0,1:T(2,128)S(1)} %multiply_add_fusion, s32[16,2,8]{2,1,0:T(2,128)S(1)} %bitcast.122), kind=kOutput, calls=%fused_computation.1 | convolution fusion | flops 464593920 | bytes 14353552 | tf_op jit(solution)/shard_map/xbkqc,aqycz->xbkayz/dot_general | solution.py:117
  91.8 4.4 %copy.133 = f32[3,16,64,2,128]{4,3,2,1,0:T(2,128)} copy(f32[3,16,64,2,128]{4,2,0,3,1:T(8,128)S(1)} %fusion.14) | data formatting | bytes 6291456 | tf_op jit(solution)/shard_map/xbkayz,kzw->axybw/transpose | solution.py:120
  96.2 5.5 %reshape.196 = f32[3,16,64,256]{3,2,1,0:T(8,128)} reshape(f32[3,16,64,2,128]{4,3,2,1,0:T(2,128)} %copy.133) | data formatting | bytes 6291456 | tf_op jit(solution)/shard_map/reshape | solution.py:123
  106.7 10.1 %all-to-all-start.1 = ((bf16[128,2,3,2048]{3,1,2,0:T(2,128)(2,1)}), bf16[128,2,3,2048]{3,1,2,0:T(2,128)(2,1)}, u32[]{:S(2)}, u32[]{:S(2)}) async-start(bf16[128,2,3,2048]{3,1,2,0:T(2,128)(2,1)} %copy.136), calls=%async_computation.1 | async-start | bytes 6291456 | tf_op jit(solution)/shard_map/all_to_all | solution.py:176
  116.8 5.8 %copy.122 = bf16[128,2,3,2048]{3,1,0,2:T(2,128)(2,1)} copy(bf16[128,2,3,2048]{3,1,2,0:T(2,128)(2,1)} %all-to-all-done) | data formatting | bytes 6291456 | tf_op jit(solution)/shard_map/all_to_all | solution.py:176
  122.7 5.7 %reshape.195 = bf16[256,3,2048]{2,0,1:T(8,128)(2,1)} reshape(bf16[128,2,3,2048]{3,1,0,2:T(2,128)(2,1)} %copy.122) | data formatting | bytes 6291456 | tf_op jit(solution)/shard_map/reshape | solution.py:183
  128.4 4.0 %fusion.4 = (f32[2048,128]{1,0:T(8,128)}, bf16[3,2048,128]{2,1,0:T(8,128)(2,1)S(1)}) fusion(bf16[256,3,2048]{2,0,1:T(8,128)(2,1)} %reshape.195, s32[128]{0:T(128)S(1)} %copy-done.8), kind=kOutput, calls=%fused_computation.12 | convolution fusion | flops 405569536 | bytes 5767680 | tf_op jit(solution)/shard_map/jr,rcb->cjb/dot_general | solution.py:184
  142.1 3.8 %bitcast_multiply_fusion.1 = (f32[16,64,256]{2,1,0:T(8,128)}, f32[16,64,256]{2,1,0:T(8,128)}) fusion(f32[16,64,256]{2,1,0:T(8,128)} %mul.349, f32[3,16,64,256]{3,2,1,0:T(8,128)S(1)} %copy-done.1, f32[16,64,80]{2,1,0:T(8,128)} %bitcast.121, f32[80]{0:T(128)S(1)} %get-tuple-element.30), kind=kOutput, calls=%fused_computation.52 | convolution fusion | flops 252526592 | bytes 4522304 | tf_op jit(solution)/shard_map/dot_general | solution.py:65
  151.6 14.2 %fusion.61 = (bf16[3,16,64,256]{3,2,1,0:T(8,128)(2,1)}, f32[3,16,64,256]{3,2,1,0:T(8,128)S(1)}) fusion(f32[16]{0:T(128)S(1)} %broadcast_select_fusion, f32[16,64,256]{2,1,0:T(8,128)} %get-tuple-element.35, f32[3]{0:T(128)S(1)} %compare_convert_fusion, f32[3,16,64,256]{3,2,1,0:T(8,128)} %param.11, f32[3,16,64,256]{3,2,1,0:T(8,128)} %reshape.196, ...), kind=kLoop, calls=%fused_computation.120 | loop fusion | flops 23592960 | bytes 26562636 | tf_op jit(solution)/shard_map/convert.6
  166.6 3.8 %fusion.63 = (f32[3,16,64,255]{3,2,1,0:T(8,128)}, f32[3,16,64,255]{3,2,1,0:T(8,128)}) fusion(f32[3,16,64,256]{3,2,1,0:T(8,128)S(1)} %get-tuple-element.3), kind=kLoop, calls=%fused_computation.122 | loop fusion | bytes 12533760 | tf_op jit(solution)/shard_map/slice | solution.py:96
  170.4 5.8 %copy.137 = bf16[128,2,3,2048]{3,1,0,2:T(2,128)(2,1)} copy(bf16[128,2,3,2048]{3,1,2,0:T(2,128)(2,1)} %all-to-all-done.1) | data formatting | bytes 6291456 | tf_op jit(solution)/shard_map/all_to_all | solution.py:176
  176.2 5.7 %reshape.198 = bf16[256,3,2048]{2,0,1:T(8,128)(2,1)} reshape(bf16[128,2,3,2048]{3,1,0,2:T(2,128)(2,1)} %copy.137) | data formatting | bytes 6291456 | tf_op jit(solution)/shard_map/reshape | solution.py:183
  181.9 4.0 %fusion.5 = (f32[2048,128]{1,0:T(8,128)}, bf16[3,2048,128]{2,1,0:T(8,128)(2,1)S(1)}) fusion(bf16[256,3,2048]{2,0,1:T(8,128)(2,1)} %reshape.198, s32[128]{0:T(128)S(1)} %copy-done.8), kind=kOutput, calls=%fused_computation.13 | convolution fusion | flops 405569536 | bytes 5767680 | tf_op jit(solution)/shard_map/jr,rcb->cjb/dot_general | solution.py:184
  204.0 67.2 %psum.16 = f32[80]{0:T(128)S(1)} all-reduce(f32[80]{0:T(128)S(1)} %select_add_fusion), channel_id=1, replica_groups=mesh['gx'=64,'gy'=2] {'gx','gy'}, use_global_device_ids=true, to_apply=%region_6.7 | all-reduce | flops 80 | bytes 640 | tf_op jit(solution)/shard_map/psum | solution.py:200
  284.6 3.5 %concatenate.83 = bf16[3,16,64,2,128]{4,3,2,1,0:T(2,128)(2,1)} reshape(bf16[3,16,64,256]{3,2,1,0:T(8,128)(2,1)} %get-tuple-element.2) | data formatting | bytes 3145728 | tf_op jit(solution)/shard_map/concatenate | solution.py:27
  288.1 4.4 %copy.144 = bf16[3,16,64,2,128]{4,1,3,2,0:T(8,128)(2,1)} copy(bf16[3,16,64,2,128]{4,3,2,1,0:T(2,128)(2,1)} %concatenate.83) | data formatting | bytes 3145728 | tf_op jit(solution)/shard_map/concatenate | solution.py:27
  314.1 5.6 %bitcast_convert_fusion = bf16[16,2,8,3,64,128]{5,2,4,3,1,0:T(8,128)(2,1)S(1)} fusion(bf16[3,1,64,2,128]{4,1,3,2,0:T(2,128)(2,1)} %concatenate.89, bf16[3,16,64,2,128]{4,1,3,2,0:T(8,128)(2,1)} %copy.144, bf16[3,1,64,2,128]{4,1,3,2,0:T(2,128)(2,1)} %concatenate.88, s32[18,2]{0,1:T(2,128)S(1)} %multiply_add_fusion, s32[16,2,8]{2,1,0:T(2,128)S(1)} %bitcast.123), kind=kOutput, calls=%fused_computation | convolution fusion | flops 464593920 | bytes 14353552 | tf_op jit(solution)/shard_map/xbkqc,aqycz->xbkayz/dot_general | solution.py:117
  319.7 3.4 %fusion.17 = f32[3,16,64,2,128]{4,2,0,3,1:T(8,128)S(1)} fusion(bf16[16,2,8,3,64,128]{5,2,4,3,1,0:T(8,128)(2,1)S(1)} %bitcast_convert_fusion, bf16[8,128,128]{2,1,0:T(8,128)(2,1)S(1)} %copy-done), kind=kOutput, calls=%fused_computation.41 | convolution fusion | flops 1610612736 | bytes 15990784 | tf_op jit(solution)/shard_map/xbkayz,kzw->axybw/dot_general | solution.py:120
  323.1 4.4 %copy.147 = f32[3,16,64,2,128]{4,3,2,1,0:T(2,128)} copy(f32[3,16,64,2,128]{4,2,0,3,1:T(8,128)S(1)} %fusion.17) | data formatting | bytes 6291456 | tf_op jit(solution)/shard_map/xbkayz,kzw->axybw/transpose | solution.py:120
  327.6 5.5 %reshape.199 = f32[3,16,64,256]{3,2,1,0:T(8,128)} reshape(f32[3,16,64,2,128]{4,3,2,1,0:T(2,128)} %copy.147) | data formatting | bytes 6291456 | tf_op jit(solution)/shard_map/reshape | solution.py:123
  333.1 9.4 %subtract_multiply_fusion = f32[3,16,64,256]{3,2,1,0:T(8,128)} fusion(f32[3,16,64,256]{3,2,1,0:T(8,128)S(1)} %get-tuple-element.3, f32[3,16,64,256]{3,2,1,0:T(8,128)} %reshape.199, f32[3,16,64,255]{3,2,1,0:T(8,128)} %get-tuple-element.17, f32[3,16,64,255]{3,2,1,0:T(8,128)} %get-tuple-element.16, f32[3,18,1,256]{3,2,1,0:T(1,128)} %collective-permute-done.6, ...), kind=kLoop, calls=%fused_computation.26 | loop fusion | flops 25952256 | bytes 21450828 | tf_op jit(solution)/shard_map/mul | solution.py:128
  (113 shorter events, 99.4 us)
Async XLA Ops:
  0.6 87.7 %copy-start = (bf16[8,128,128]{2,1,0:T(8,128)(2,1)S(1)}, bf16[8,128,128]{2,1,0:T(8,128)(2,1)}, u32[]{:S(2)}) copy-start(bf16[8,128,128]{2,1,0:T(8,128)(2,1)} %param.16) | copy-start | bytes 786436
  15.6 11.9 %copy-start.1 = (f32[3,16,64,256]{3,2,1,0:T(8,128)S(1)}, f32[3,16,64,256]{3,2,1,0:T(8,128)}, u32[]{:S(2)}) copy-start(f32[3,16,64,256]{3,2,1,0:T(8,128)} %param.11) | copy-start | bytes 9437188
  15.6 91.2 %all-to-all-start = ((bf16[128,2,3,2048]{3,1,2,0:T(2,128)(2,1)}), bf16[128,2,3,2048]{3,1,2,0:T(2,128)(2,1)}, u32[]{:S(2)}, u32[]{:S(2)}) async-start(bf16[128,2,3,2048]{3,1,2,0:T(2,128)(2,1)} %copy.121), calls=%async_computation | async-start | bytes 6291456 | tf_op jit(solution)/shard_map/all_to_all | solution.py:176
  28.3 38.3 %collective-permute-start.1 = (f32[3,1,64,256]{3,2,1,0:T(8,128)}, f32[3,1,64,256]{3,2,1,0:T(8,128)}, u32[]{:S(2)}, u32[]{:S(2)}) collective-permute-start(f32[3,1,64,256]{3,2,1,0:T(8,128)} %get-tuple-element.24), channel_id=1, source_target_pairs={{0,2},{2,4},{4,6},{6,8},{8,10},{10,12},{12,14},{14,16},{16,18},{18... | collective-permute-start | bytes 589832 | tf_op jit(solution)/shard_map/ppermute | solution.py:23
  31.8 39.0 %collective-permute-start = (f32[3,1,64,256]{3,2,1,0:T(8,128)}, f32[3,1,64,256]{3,2,1,0:T(8,128)}, u32[]{:S(2)}, u32[]{:S(2)}) collective-permute-start(f32[3,1,64,256]{3,2,1,0:T(8,128)} %get-tuple-element.25), channel_id=1, source_target_pairs={{2,0},{4,2},{6,4},{8,6},{10,8},{12,10},{14,12},{16,14},{18,16},{20... | collective-permute-start | bytes 589832 | tf_op jit(solution)/shard_map/ppermute | solution.py:26
  32.0 3.8 %copy-start.6 = (bf16[2,128,3,2048]{3,1,2,0:T(8,128)(2,1)S(1)}, bf16[2,128,3,2048]{3,1,2,0:T(8,128)(2,1)}, u32[]{:S(2)}) copy-start(bf16[2,128,3,2048]{3,1,2,0:T(8,128)(2,1)} %param.12) | copy-start | bytes 9437188
  35.8 2.7 copy-start.11
  35.8 6.0 %copy-start.12 = (f32[80]{0:T(128)S(1)}, f32[80]{0:T(128)}, u32[]{:S(2)}) copy-start(f32[80]{0:T(128)} %param.18) | copy-start | bytes 964
  35.8 6.0 %copy-start.9 = (s32[80]{0:T(128)S(1)}, s32[80]{0:T(128)}, u32[]{:S(2)}) copy-start(s32[80]{0:T(128)} %param.20) | copy-start | bytes 964
  35.8 6.0 %copy-start.10 = (f32[80]{0:T(128)S(1)}, f32[80]{0:T(128)}, u32[]{:S(2)}) copy-start(f32[80]{0:T(128)} %param.17) | copy-start | bytes 964
  35.8 9.8 %copy-start.7 = (s32[32,8]{0,1:T(8,128)S(1)}, s32[32,8]{0,1:T(8,128)}, u32[]{:S(2)}) copy-start(s32[32,8]{0,1:T(8,128)} %param.15) | copy-start | bytes 3076
  51.7 5.7 %copy-start.13 = (s32[128]{0:T(128)S(1)}, s32[128]{0:T(128)}, u32[]{:S(2)}) copy-start(s32[128]{0:T(128)} %param.21) | copy-start | bytes 1540
  103.7 48.0 %collective-permute-start.2 = (f32[3,18,1,256]{3,2,1,0:T(1,128)}, f32[3,18,1,256]{3,2,1,0:T(1,128)S(1)}, u32[]{:S(2)}, u32[]{:S(2)}) collective-permute-start(f32[3,18,1,256]{3,2,1,0:T(1,128)} %get-tuple-element.6), channel_id=1, source_target_pairs={{1,0},{0,1},{3,2},{2,3},{5,4},{4,5},{7,6},{6,7},{9,8},{8,9},{11,10... | collective-permute-start | bytes 165896 | tf_op jit(solution)/shard_map/ppermute | solution.py:26
  106.7 44.9 %collective-permute-start.3 = (f32[3,18,1,256]{3,2,1,0:T(1,128)}, f32[3,18,1,256]{3,2,1,0:T(1,128)}, u32[]{:S(2)}, u32[]{:S(2)}) collective-permute-start(f32[3,18,1,256]{3,2,1,0:T(1,128)} %get-tuple-element.7), channel_id=1, source_target_pairs={{0,1},{1,0},{2,3},{3,2},{4,5},{5,4},{6,7},{7,6},{8,9},{9,8},{10,11... | collective-permute-start | bytes 165896 | tf_op jit(solution)/shard_map/ppermute | solution.py:23
  106.7 63.7 %all-to-all-start.1 = ((bf16[128,2,3,2048]{3,1,2,0:T(2,128)(2,1)}), bf16[128,2,3,2048]{3,1,2,0:T(2,128)(2,1)}, u32[]{:S(2)}, u32[]{:S(2)}) async-start(bf16[128,2,3,2048]{3,1,2,0:T(2,128)(2,1)} %copy.136), calls=%async_computation.1 | async-start | bytes 6291456 | tf_op jit(solution)/shard_map/all_to_all | solution.py:176
  122.7 5.7 %copy-start.8 = (s32[128]{0:T(128)S(1)}, s32[128]{0:T(128)}, u32[]{:S(2)}) copy-start(s32[128]{0:T(128)} %param.14) | copy-start | bytes 1540
  145.9 2.8 copy-start.4
  147.5 2.6 copy-start.5
  193.3 1.4 copy-start.2
  200.9 1.7 copy-start.3
  271.2 36.7 %collective-permute-start.4 = (f32[3,1,64,256]{3,2,1,0:T(8,128)}, f32[3,1,64,256]{3,2,1,0:T(8,128)}, u32[]{:S(2)}, u32[]{:S(2)}) collective-permute-start(f32[3,1,64,256]{3,2,1,0:T(8,128)} %get-tuple-element.19), channel_id=1, source_target_pairs={{2,0},{4,2},{6,4},{8,6},{10,8},{12,10},{14,12},{16,14},{18,16},{20... | collective-permute-start | bytes 589832 | tf_op jit(solution)/shard_map/ppermute | solution.py:26
  272.0 35.8 %collective-permute-start.5 = (f32[3,1,64,256]{3,2,1,0:T(8,128)}, f32[3,1,64,256]{3,2,1,0:T(8,128)}, u32[]{:S(2)}, u32[]{:S(2)}) collective-permute-start(f32[3,1,64,256]{3,2,1,0:T(8,128)} %get-tuple-element.18), channel_id=1, source_target_pairs={{0,2},{2,4},{4,6},{6,8},{8,10},{10,12},{12,14},{14,16},{16,18},{18... | collective-permute-start | bytes 589832 | tf_op jit(solution)/shard_map/ppermute | solution.py:23
  309.3 23.7 %collective-permute-start.6 = (f32[3,18,1,256]{3,2,1,0:T(1,128)}, f32[3,18,1,256]{3,2,1,0:T(1,128)}, u32[]{:S(2)}, u32[]{:S(2)}) collective-permute-start(f32[3,18,1,256]{3,2,1,0:T(1,128)} %get-tuple-element.5), channel_id=1, source_target_pairs={{1,0},{0,1},{3,2},{2,3},{5,4},{4,5},{7,6},{6,7},{9,8},{8,9},{11,10... | collective-permute-start | bytes 165896 | tf_op jit(solution)/shard_map/ppermute | solution.py:26
  309.3 23.7 %collective-permute-start.7 = (f32[3,18,1,256]{3,2,1,0:T(1,128)}, f32[3,18,1,256]{3,2,1,0:T(1,128)}, u32[]{:S(2)}, u32[]{:S(2)}) collective-permute-start(f32[3,18,1,256]{3,2,1,0:T(1,128)} %get-tuple-element.4), channel_id=1, source_target_pairs={{0,1},{1,0},{2,3},{3,2},{4,5},{5,4},{6,7},{7,6},{8,9},{9,8},{10,11... | collective-permute-start | bytes 165896 | tf_op jit(solution)/shard_map/ppermute | solution.py:23
where the time goes:
time: 349 us; the launch traced here: 343 us
  local copies, waits for them, and re-layouts  138 us (40%)
  blocking collectives  67.2 us (19%)
  other arithmetic  54.9 us (16%)
  matrix products  39 us (11%)
  starting transfers between devices  33.5 us (10%)
  waiting for transfers between devices  8.97 us (3%)
    psum x1, blocking collectives, shards(): gradient_sum = gradient_sum + lax.psum(gradient_part, ('gx', 'gy'))  67.2 us
    all_to_all x2, starting transfers between devices, shards(): lax.all_to_all(packed.reshape((tile_count, CAP) + block_shape), ('gx', 'g...  22 us
    reshape x4, local copies, waits for them, and re-layouts, shards(): packed.reshape((tile_count, CAP) + block_shape)  20.1 us
    concatenate x8, local copies, waits for them, and re-layouts, padded(): block = jnp.concatenate([low, block, high], axis=dim)  19.5 us
    another operation x3, other arithmetic  16.1 us
    all_to_all x2, local copies, waits for them, and re-layouts, shards(): lax.all_to_all(packed.reshape((tile_count, CAP) + block_shape), ('gx', 'g...  11.7 us
    reshape x2, local copies, waits for them, and re-layouts, shards(): arrived = arrived.reshape((tile_count * CAP,) + block_shape)  11.4 us
    dot_general x2, matrix products, advance(): jnp.einsum('xbkqc,aqycz->xbkayz', selector, planes, preferred_element_typ...  11.2 us
  transfers between devices with their start and end apart: 10, of which 1 were waited for; matrix products, arithmetic and copies ran while one was open for 50% of the time, Pallas kernels for 0%

commit v1 on v0

--- a/solution.py
+++ b/solution.py
@@ -197,7 +197,7 @@
             drag_field,
             fringe_scale,
         )
-        gradient_sum = gradient_sum + lax.psum(gradient_part, ("gx", "gy"))
+        gradient_sum = gradient_sum + jnp.sum(lax.all_gather(gradient_part, ("gx", "gy")), axis=0)
     cosine = jnp.cos(yaw_angle)
     sine = jnp.sin(yaw_angle)
     control_gradient = jnp.stack(

time: 349 us -> 420 us (1.20)
  waiting for transfers between devices: 8.97 us -> 131 us
  blocking collectives: 67.2 us -> 0 us
  between operations: 1.2 us -> 14.6 us
    unnamed x0 -> x2, waiting for transfers between devices: none -> 118 us
    psum x1 -> x0, blocking collectives: 67.2 us -> none  [shards(): gradient_sum = gradient_sum + lax.psum(gradient_part, ('gx', 'gy'))]
  transfers between devices with their start and end apart: 10 -> 11, of which waited for: 1 -> 2; matrix products, arithmetic and copies ran while one was open for 50% -> 44% of each run, Pallas kernels for 0% -> 0%
where the time goes in v1:
time: 420 us; the launch traced here: 414 us
  local copies, waits for them, and re-layouts  141 us (34%)
  waiting for transfers between devices  131 us (31%)
  other arithmetic  54.9 us (13%)
  matrix products  39 us (9%)
  starting transfers between devices  33.4 us (8%)
  between operations  14.6 us (3%)
    unnamed x2, waiting for transfers between devices  118 us
    all_to_all x2, starting transfers between devices, shards(): lax.all_to_all(packed.reshape((tile_count, CAP) + block_shape), ('gx', 'g...  21.4 us
    reshape x4, local copies, waits for them, and re-layouts, shards(): packed.reshape((tile_count, CAP) + block_shape)  20.2 us
    concatenate x8, local copies, waits for them, and re-layouts, padded(): block = jnp.concatenate([low, block, high], axis=dim)  19.6 us
    another operation x3, other arithmetic  16 us
    ppermute x4, waiting for transfers between devices, padded(): lax.ppermute(lax.slice_in_dim(block, block.shape[dim] - width, None, axis...  12.6 us
    reshape x2, local copies, waits for them, and re-layouts, shards(): arrived = arrived.reshape((tile_count * CAP,) + block_shape)  11.8 us
    all_to_all x2, local copies, waits for them, and re-layouts, shards(): lax.all_to_all(packed.reshape((tile_count, CAP) + block_shape), ('gx', 'g...  11.7 us
  transfers between devices with their start and end apart: 11, of which 2 were waited for; matrix products, arithmetic and copies ran while one was open for 44% of the time, Pallas kernels for 0%

profile of v1, /device:TPU:1, one launch (start us, length us, event | category | flops | bytes accessed | tf_op | source)
XLA Modules:
  0.0 413.7 jit_solution(1494674230278963952)
XLA Ops:
  9.6 4.0 convolution_convert_fusion.1
  13.7 4.6 %reshape.194 = bf16[128,2,3,2048]{3,1,0,2:T(2,128)(2,1)S(1)} reshape(bf16[256,3,2048]{2,0,1:T(8,128)(2,1)} %convolution_convert_fusion.1) | data formatting | bytes 6291456 | tf_op jit(solution)/shard_map/reshape | solution.py:177
  18.3 3.8 copy.121
  22.1 11.9 %all-to-all-start = ((bf16[128,2,3,2048]{3,1,2,0:T(2,128)(2,1)}), bf16[128,2,3,2048]{3,1,2,0:T(2,128)(2,1)}, u32[]{:S(2)}, u32[]{:S(2)}) async-start(bf16[128,2,3,2048]{3,1,2,0:T(2,128)(2,1)} %copy.121), calls=%async_computation | async-start | bytes 6291456 | tf_op jit(solution)/shard_map/all_to_all | solution.py:176
  34.8 3.5 collective-permute-start.1
  38.5 3.9 fusion.65
  48.5 6.0 %reshape.197 = bf16[128,2,3,2048]{3,1,0,2:T(2,128)(2,1)} reshape(bf16[256,3,2048]{2,0,1:T(8,128)(2,1)} %convolution_convert_fusion) | data formatting | bytes 6291456 | tf_op jit(solution)/shard_map/reshape | solution.py:177
  54.5 5.7 %copy.136 = bf16[128,2,3,2048]{3,1,2,0:T(2,128)(2,1)} copy(bf16[128,2,3,2048]{3,1,0,2:T(2,128)(2,1)} %reshape.197) | data formatting | bytes 6291456 | tf_op jit(solution)/shard_map/reshape | solution.py:177
  60.5 12.6 %collective-permute-done.1 = f32[3,1,64,256]{3,2,1,0:T(8,128)} collective-permute-done((f32[3,1,64,256]{3,2,1,0:T(8,128)}, f32[3,1,64,256]{3,2,1,0:T(8,128)}, u32[]{:S(2)}, u32[]{:S(2)}) %collective-permute-start.1) | collective-permute-done | bytes 196640 | tf_op jit(solution)/shard_map/ppermute | solution.py:23
  80.8 3.5 concatenate.72
  84.3 4.4 %copy.130 = bf16[3,16,64,2,128]{4,1,3,2,0:T(8,128)(2,1)} copy(bf16[3,16,64,2,128]{4,3,2,1,0:T(2,128)(2,1)} %concatenate.72) | data formatting | bytes 3145728 | tf_op jit(solution)/shard_map/concatenate | solution.py:27
  89.4 5.6 %bitcast_convert_fusion.1 = bf16[16,2,8,3,64,128]{5,2,4,3,1,0:T(8,128)(2,1)S(1)} fusion(bf16[3,1,64,2,128]{4,1,3,2,0:T(2,128)(2,1)} %concatenate.87, bf16[3,16,64,2,128]{4,1,3,2,0:T(8,128)(2,1)} %copy.130, bf16[3,1,64,2,128]{4,1,3,2,0:T(2,128)(2,1)} %concatenate.86, s32[18,2]{0,1:T(2,128)S(1)} %multiply_add_fusion, s32[16,2,8]{2,1,0:T(2,128)S(1)} %bitcast.122), kind=kOutput, calls=%fused_computation.1 | convolution fusion | flops 464593920 | bytes 14353552 | tf_op jit(solution)/shard_map/xbkqc,aqycz->xbkayz/dot_general | solution.py:117
  98.4 4.4 %copy.133 = f32[3,16,64,2,128]{4,3,2,1,0:T(2,128)} copy(f32[3,16,64,2,128]{4,2,0,3,1:T(8,128)S(1)} %fusion.14) | data formatting | bytes 6291456 | tf_op jit(solution)/shard_map/xbkayz,kzw->axybw/transpose | solution.py:120
  102.8 5.5 %reshape.196 = f32[3,16,64,256]{3,2,1,0:T(8,128)} reshape(f32[3,16,64,2,128]{4,3,2,1,0:T(2,128)} %copy.133) | data formatting | bytes 6291456 | tf_op jit(solution)/shard_map/reshape | solution.py:123
  113.2 9.5 %all-to-all-start.1 = ((bf16[128,2,3,2048]{3,1,2,0:T(2,128)(2,1)}), bf16[128,2,3,2048]{3,1,2,0:T(2,128)(2,1)}, u32[]{:S(2)}, u32[]{:S(2)}) async-start(bf16[128,2,3,2048]{3,1,2,0:T(2,128)(2,1)} %copy.136), calls=%async_computation.1 | async-start | bytes 6291456 | tf_op jit(solution)/shard_map/all_to_all | solution.py:176
  122.8 5.8 %copy.122 = bf16[128,2,3,2048]{3,1,0,2:T(2,128)(2,1)} copy(bf16[128,2,3,2048]{3,1,2,0:T(2,128)(2,1)} %all-to-all-done) | data formatting | bytes 6291456 | tf_op jit(solution)/shard_map/all_to_all | solution.py:176
  128.7 6.1 %reshape.195 = bf16[256,3,2048]{2,0,1:T(8,128)(2,1)} reshape(bf16[128,2,3,2048]{3,1,0,2:T(2,128)(2,1)} %copy.122) | data formatting | bytes 6291456 | tf_op jit(solution)/shard_map/reshape | solution.py:183
  134.8 4.0 fusion.4
  159.2 3.8 bitcast_multiply_fusion.1
  168.8 14.1 %fusion.61 = (bf16[3,16,64,256]{3,2,1,0:T(8,128)(2,1)}, f32[3,16,64,256]{3,2,1,0:T(8,128)S(1)}) fusion(f32[16]{0:T(128)S(1)} %broadcast_select_fusion, f32[16,64,256]{2,1,0:T(8,128)} %get-tuple-element.39, f32[3]{0:T(128)S(1)} %compare_convert_fusion, f32[3,16,64,256]{3,2,1,0:T(8,128)} %param.11, f32[3,16,64,256]{3,2,1,0:T(8,128)} %reshape.196, ...), kind=kLoop, calls=%fused_computation.121 | loop fusion | flops 23592960 | bytes 26562636 | tf_op jit(solution)/shard_map/convert.6
  183.6 3.8 fusion.63
  187.5 5.8 %copy.137 = bf16[128,2,3,2048]{3,1,0,2:T(2,128)(2,1)} copy(bf16[128,2,3,2048]{3,1,2,0:T(2,128)(2,1)} %all-to-all-done.1) | data formatting | bytes 6291456 | tf_op jit(solution)/shard_map/all_to_all | solution.py:176
  193.3 5.7 %reshape.198 = bf16[256,3,2048]{2,0,1:T(8,128)(2,1)} reshape(bf16[128,2,3,2048]{3,1,0,2:T(2,128)(2,1)} %copy.137) | data formatting | bytes 6291456 | tf_op jit(solution)/shard_map/reshape | solution.py:183
  199.1 4.0 fusion.5
  227.5 3.5 concatenate.83
  231.0 4.4 %copy.144 = bf16[3,16,64,2,128]{4,1,3,2,0:T(8,128)(2,1)} copy(bf16[3,16,64,2,128]{4,3,2,1,0:T(2,128)(2,1)} %concatenate.83) | data formatting | bytes 3145728 | tf_op jit(solution)/shard_map/concatenate | solution.py:27
  250.1 118.2 %all-reduce.9.cloned.1.call-done = (f32[10240]{0:T(1024)}, f32[10240]{0:T(1024)}) async-done(((f32[10240]{0:T(1024)}, f32[10240]{0:T(1024)}), (f32[10240]{0:T(1024)}, f32[10240]{0:T(1024)})) %all-reduce.9.cloned.1.call-update) | async-done | bytes 81936
  378.3 5.6 %bitcast_convert_fusion = bf16[16,2,8,3,64,128]{5,2,4,3,1,0:T(8,128)(2,1)S(1)} fusion(bf16[3,1,64,2,128]{4,1,3,2,0:T(2,128)(2,1)} %concatenate.89, bf16[3,16,64,2,128]{4,1,3,2,0:T(8,128)(2,1)} %copy.144, bf16[3,1,64,2,128]{4,1,3,2,0:T(2,128)(2,1)} %concatenate.88, s32[18,2]{0,1:T(2,128)S(1)} %copy-done.10, s32[16,2,8]{2,1,0:T(2,128)S(1)} %bitcast.123), kind=kOutput, calls=%fused_computation | convolution fusion | flops 464593920 | bytes 14353552 | tf_op jit(solution)/shard_map/xbkqc,aqycz->xbkayz/dot_general | solution.py:117
  383.9 3.4 fusion.17
  387.3 4.4 %copy.147 = f32[3,16,64,2,128]{4,3,2,1,0:T(2,128)} copy(f32[3,16,64,2,128]{4,2,0,3,1:T(8,128)S(1)} %fusion.17) | data formatting | bytes 6291456 | tf_op jit(solution)/shard_map/xbkayz,kzw->axybw/transpose | solution.py:120
  391.7 5.5 %reshape.199 = f32[3,16,64,256]{3,2,1,0:T(8,128)} reshape(f32[3,16,64,2,128]{4,3,2,1,0:T(2,128)} %copy.147) | data formatting | bytes 6291456 | tf_op jit(solution)/shard_map/reshape | solution.py:123
  397.2 9.4 %subtract_multiply_fusion = f32[3,16,64,256]{3,2,1,0:T(8,128)} fusion(f32[3,16,64,256]{3,2,1,0:T(8,128)S(1)} %get-tuple-element.5, f32[3,16,64,256]{3,2,1,0:T(8,128)} %reshape.199, f32[3,16,64,255]{3,2,1,0:T(8,128)} %get-tuple-element.19, f32[3,16,64,255]{3,2,1,0:T(8,128)} %get-tuple-element.18, f32[3,18,1,256]{3,2,1,0:T(1,128)} %collective-permute-done.6, ...), kind=kLoop, calls=%fused_computation.26 | loop fusion | flops 25952256 | bytes 21450828 | tf_op jit(solution)/shard_map/mul | solution.py:128
  (139 shorter events, 102.5 us)
Async XLA Ops:
  7.2 87.8 %copy-start = (bf16[8,128,128]{2,1,0:T(8,128)(2,1)S(1)}, bf16[8,128,128]{2,1,0:T(8,128)(2,1)}, u32[]{:S(2)}) copy-start(bf16[8,128,128]{2,1,0:T(8,128)(2,1)} %param.16) | copy-start | bytes 786436
  22.1 11.9 %copy-start.1 = (f32[3,16,64,256]{3,2,1,0:T(8,128)S(1)}, f32[3,16,64,256]{3,2,1,0:T(8,128)}, u32[]{:S(2)}) copy-start(f32[3,16,64,256]{3,2,1,0:T(8,128)} %param.11) | copy-start | bytes 9437188
  22.1 91.2 %all-to-all-start = ((bf16[128,2,3,2048]{3,1,2,0:T(2,128)(2,1)}), bf16[128,2,3,2048]{3,1,2,0:T(2,128)(2,1)}, u32[]{:S(2)}, u32[]{:S(2)}) async-start(bf16[128,2,3,2048]{3,1,2,0:T(2,128)(2,1)} %copy.121), calls=%async_computation | async-start | bytes 6291456 | tf_op jit(solution)/shard_map/all_to_all | solution.py:176
  34.8 38.2 %collective-permute-start.1 = (f32[3,1,64,256]{3,2,1,0:T(8,128)}, f32[3,1,64,256]{3,2,1,0:T(8,128)}, u32[]{:S(2)}, u32[]{:S(2)}) collective-permute-start(f32[3,1,64,256]{3,2,1,0:T(8,128)} %get-tuple-element.26), channel_id=1, source_target_pairs={{0,2},{2,4},{4,6},{6,8},{8,10},{10,12},{12,14},{14,16},{16,18},{18... | collective-permute-start | bytes 589832 | tf_op jit(solution)/shard_map/ppermute | solution.py:23
  38.4 39.0 %collective-permute-start = (f32[3,1,64,256]{3,2,1,0:T(8,128)}, f32[3,1,64,256]{3,2,1,0:T(8,128)}, u32[]{:S(2)}, u32[]{:S(2)}) collective-permute-start(f32[3,1,64,256]{3,2,1,0:T(8,128)} %get-tuple-element.27), channel_id=1, source_target_pairs={{2,0},{4,2},{6,4},{8,6},{10,8},{12,10},{14,12},{16,14},{18,16},{20... | collective-permute-start | bytes 589832 | tf_op jit(solution)/shard_map/ppermute | solution.py:26
  38.5 3.9 copy-start.6
  42.4 2.6 copy-start.20
  42.4 126.3 %copy-start.13 = (f32[3]{0:T(128)}, f32[3]{0:T(128)S(1)}, u32[]{:S(2)}) copy-start(f32[3]{0:T(128)S(1)} %compare_convert_fusion) | copy-start | bytes 40
  42.4 5.9 %copy-start.21 = (f32[80]{0:T(128)S(1)}, f32[80]{0:T(128)}, u32[]{:S(2)}) copy-start(f32[80]{0:T(128)} %param.18) | copy-start | bytes 964
  42.4 6.0 %copy-start.11 = (s32[32,8]{0,1:T(8,128)S(1)}, s32[32,8]{0,1:T(8,128)}, u32[]{:S(2)}) copy-start(s32[32,8]{0,1:T(8,128)} %param.15) | copy-start | bytes 3076
  48.4 100.4 %copy-start.19 = (f32[80]{0:T(128)}, f32[80]{0:T(128)S(1)}, u32[]{:S(2)}) copy-start(f32[80]{0:T(128)S(1)} %cos.4) | copy-start | bytes 964
  54.5 5.7 %copy-start.22 = (s32[128]{0:T(128)S(1)}, s32[128]{0:T(128)}, u32[]{:S(2)}) copy-start(s32[128]{0:T(128)} %param.21) | copy-start | bytes 1540
  60.3 29.1 %copy-start.9 = (s32[18,2]{0,1:T(2,128)}, s32[18,2]{0,1:T(2,128)S(1)}, u32[]{:S(2)}) copy-start(s32[18,2]{0,1:T(2,128)S(1)} %multiply_add_fusion) | copy-start | bytes 436
  60.5 108.3 %copy-start.15 = (f32[16]{0:T(128)}, f32[16]{0:T(128)S(1)}, u32[]{:S(2)}) copy-start(f32[16]{0:T(128)S(1)} %broadcast_select_fusion) | copy-start | bytes 196
  110.2 58.6 %collective-permute-start.2 = (f32[3,18,1,256]{3,2,1,0:T(1,128)}, f32[3,18,1,256]{3,2,1,0:T(1,128)S(1)}, u32[]{:S(2)}, u32[]{:S(2)}) collective-permute-start(f32[3,18,1,256]{3,2,1,0:T(1,128)} %get-tuple-element.8), channel_id=1, source_target_pairs={{1,0},{0,1},{3,2},{2,3},{5,4},{4,5},{7,6},{6,7},{9,8},{8,9},{11,10... | collective-permute-start | bytes 165896 | tf_op jit(solution)/shard_map/ppermute | solution.py:26
  113.2 55.5 %collective-permute-start.3 = (f32[3,18,1,256]{3,2,1,0:T(1,128)}, f32[3,18,1,256]{3,2,1,0:T(1,128)}, u32[]{:S(2)}, u32[]{:S(2)}) collective-permute-start(f32[3,18,1,256]{3,2,1,0:T(1,128)} %get-tuple-element.9), channel_id=1, source_target_pairs={{0,1},{1,0},{2,3},{3,2},{4,5},{5,4},{6,7},{7,6},{8,9},{9,8},{10,11... | collective-permute-start | bytes 165896 | tf_op jit(solution)/shard_map/ppermute | solution.py:23
  113.2 74.2 %all-to-all-start.1 = ((bf16[128,2,3,2048]{3,1,2,0:T(2,128)(2,1)}), bf16[128,2,3,2048]{3,1,2,0:T(2,128)(2,1)}, u32[]{:S(2)}, u32[]{:S(2)}) async-start(bf16[128,2,3,2048]{3,1,2,0:T(2,128)(2,1)} %copy.136), calls=%async_computation.1 | async-start | bytes 6291456 | tf_op jit(solution)/shard_map/all_to_all | solution.py:176
  122.8 245.6 %all-reduce.9.cloned.1.call-start = ((), (), s32[]{:S(2)}) async-start(), calls=%async_computation.2 | async-start | bytes 163840
  128.7 6.1 %copy-start.12 = (s32[128]{0:T(128)S(1)}, s32[128]{0:T(128)}, u32[]{:S(2)}) copy-start(s32[128]{0:T(128)} %param.14) | copy-start | bytes 1540
  143.7 5.1 %copy-start.17 = (s32[80]{0:T(128)S(1)}, s32[80]{0:T(128)}, u32[]{:S(2)}) copy-start(s32[80]{0:T(128)} %param.20) | copy-start | bytes 964
  143.7 5.1 %copy-start.18 = (f32[80]{0:T(128)S(1)}, f32[80]{0:T(128)}, u32[]{:S(2)}) copy-start(f32[80]{0:T(128)} %param.17) | copy-start | bytes 964
  146.1 1.4 copy-start.2
  149.0 10.2 %copy-start.7 = (f32[10240]{0:T(1024)}, f32[10240]{0:T(1024)S(1)}, u32[]{:S(2)}) copy-start(f32[10240]{0:T(1024)S(1)} %get-tuple-element.37) | copy-start | bytes 122884
  162.9 2.8 copy-start.4
  164.6 2.7 copy-start.5
  213.0 159.0 %collective-permute-start.4 = (f32[3,1,64,256]{3,2,1,0:T(8,128)}, f32[3,1,64,256]{3,2,1,0:T(8,128)}, u32[]{:S(2)}, u32[]{:S(2)}) collective-permute-start(f32[3,1,64,256]{3,2,1,0:T(8,128)} %get-tuple-element.21), channel_id=1, source_target_pairs={{2,0},{4,2},{6,4},{8,6},{10,8},{12,10},{14,12},{16,14},{18,16},{20... | collective-permute-start | bytes 589832 | tf_op jit(solution)/shard_map/ppermute | solution.py:26
  214.2 157.8 %collective-permute-start.5 = (f32[3,1,64,256]{3,2,1,0:T(8,128)}, f32[3,1,64,256]{3,2,1,0:T(8,128)}, u32[]{:S(2)}, u32[]{:S(2)}) collective-permute-start(f32[3,1,64,256]{3,2,1,0:T(8,128)} %get-tuple-element.20), channel_id=1, source_target_pairs={{0,2},{2,4},{4,6},{6,8},{8,10},{10,12},{12,14},{14,16},{16,18},{18... | collective-permute-start | bytes 589832 | tf_op jit(solution)/shard_map/ppermute | solution.py:23
  370.6 7.6 %copy-start.10 = (s32[18,2]{0,1:T(2,128)S(1)}, s32[18,2]{0,1:T(2,128)}, u32[]{:S(2)}) copy-start(s32[18,2]{0,1:T(2,128)} %copy-done.9) | copy-start | bytes 436
  373.5 23.7 %collective-permute-start.6 = (f32[3,18,1,256]{3,2,1,0:T(1,128)}, f32[3,18,1,256]{3,2,1,0:T(1,128)}, u32[]{:S(2)}, u32[]{:S(2)}) collective-permute-start(f32[3,18,1,256]{3,2,1,0:T(1,128)} %get-tuple-element.7), channel_id=1, source_target_pairs={{1,0},{0,1},{3,2},{2,3},{5,4},{4,5},{7,6},{6,7},{9,8},{8,9},{11,10... | collective-permute-start | bytes 165896 | tf_op jit(solution)/shard_map/ppermute | solution.py:26
  374.8 22.4 %collective-permute-start.7 = (f32[3,18,1,256]{3,2,1,0:T(1,128)}, f32[3,18,1,256]{3,2,1,0:T(1,128)}, u32[]{:S(2)}, u32[]{:S(2)}) collective-permute-start(f32[3,18,1,256]{3,2,1,0:T(1,128)} %get-tuple-element.6), channel_id=1, source_target_pairs={{0,1},{1,0},{2,3},{3,2},{4,5},{5,4},{6,7},{7,6},{8,9},{9,8},{10,11... | collective-permute-start | bytes 165896 | tf_op jit(solution)/shard_map/ppermute | solution.py:23
  391.7 5.5 %copy-start.14 = (f32[3]{0:T(128)S(1)}, f32[3]{0:T(128)}, u32[]{:S(2)}) copy-start(f32[3]{0:T(128)} %copy-done.13) | copy-start | bytes 40
  391.7 5.5 %copy-start.16 = (f32[16]{0:T(128)S(1)}, f32[16]{0:T(128)}, u32[]{:S(2)}) copy-start(f32[16]{0:T(128)} %copy-done.15) | copy-start | bytes 196
  (2 other events, 2.0 us)
Sparse Core Ops, SparseCore 0:
  224.9 143.4 all-reduce.8
